TPU v7x, 256 devices: a whole 4x4x8 slice. The times are simulated.
256 devices in a mesh: dish: 8 (over y, x_hi), blk: 32 (over x_lo, z, core).
Axes of the slice: x: 4 (x_hi: 2, x_lo: 2; x = x_hi * 2 + x_lo), y: 4, z: 8, core: 2. Of those that a mesh axis runs over, the one named last changes fastest.
Arguments:
- sky_data: float32 [8, 2048, 32768], P('dish', 'blk'), may hold values from -6 to 6
- eigenmodes: float32 [2048, 64], replicated, may hold values from -0.125 to 0.125
- noise_power: float32 [64, 32768], P('blk'), may hold values from 0.1 to 10
Outputs:
- cleaned: bfloat16 [8, 2048, 32768], P('dish', 'blk')
- mode_signal: float32 [8, 64, 32768], P('dish', 'blk')
All inputs are finite; a program needn't handle non-finite values.
Results may differ from a plain program's by a relative error of at most 0.0028.
Values may be sent and summed in bfloat16 or wider, within the bound.
No kernel may reach another device: no remote copies, remote signals or barrier semaphores. Data moves between devices by JAX's collectives and lax.ppermute only.
A program may use at most 128 MiB of HBM per device.

v0:
```python
import math
import jax
import jax.numpy as jnp
from jax import lax
from jax.sharding import Mesh
from jax.sharding import PartitionSpec as P

BLK = ("blk_0", "blk_1", "blk_2")
highest = lax.Precision.HIGHEST


def sent_to_all(value, axis):
    copies = jnp.broadcast_to(value, (lax.axis_size(axis), *value.shape))
    return lax.all_to_all(copies, axis, split_axis=0, concat_axis=0, tiled=True)


def taken_together(value, axis):
    return sent_to_all(value, axis).astype(jnp.float32).sum(axis=0)


def in_blocks(value, dim, size):
    before, after = (value.shape[:dim], value.shape[dim + 1 :])
    return jnp.moveaxis(value.reshape(*before, size, -1, *after), dim, 0)


def sent_and_summed(value, axis, dim):
    size = lax.axis_size(axis)
    parts = lax.all_to_all(in_blocks(value, dim, size), axis, 0, 0, tiled=True)
    return jnp.sum(parts, axis=0)


def sum_by_axis(value, axes, dim):
    far, near = axes
    parts = in_blocks(value, dim, lax.axis_size(far))
    nearer = sent_and_summed(parts, near, dim + 1)
    arrived = lax.all_to_all(nearer, far, split_axis=0, concat_axis=0, tiled=True)
    return arrived.sum(axis=0)


def dft_table(length):
    index = jnp.arange(length, dtype=jnp.int32)
    phase = (index[:, None] * index[None, :] % length).astype(jnp.float32) * (
        2.0 * math.pi / length
    )
    return (jnp.cos(phase), jnp.sin(phase))


def twist_table(rows_count, cols_count):
    total = rows_count * cols_count
    first = jnp.arange(rows_count, dtype=jnp.int32)
    second = jnp.arange(cols_count, dtype=jnp.int32)
    phase = (first[:, None] * second[None, :] % total).astype(jnp.float32) * (2.0 * math.pi / total)
    return (jnp.cos(phase), jnp.sin(phase))


def forward(series, tables):
    col_cos, col_sin, row_cos, row_sin, twist_cos, twist_sin = tables
    batch_count, length = series.shape
    grid = series.reshape(batch_count, length // 128, 128)
    inner_real = jnp.einsum("bqp,qk->bpk", grid, col_cos, precision=highest)
    inner_imag = -jnp.einsum("bqp,qk->bpk", grid, col_sin, precision=highest)
    turned_real = inner_real * twist_cos + inner_imag * twist_sin
    turned_imag = inner_imag * twist_cos - inner_real * twist_sin
    spec_real = jnp.einsum("kp,bpj->bkj", row_cos, turned_real, precision=highest) + jnp.einsum(
        "kp,bpj->bkj", row_sin, turned_imag, precision=highest
    )
    spec_imag = jnp.einsum("kp,bpj->bkj", row_cos, turned_imag, precision=highest) - jnp.einsum(
        "kp,bpj->bkj", row_sin, turned_real, precision=highest
    )
    return (spec_real, spec_imag)


def inverse(held_real, held_imag, tables, length):
    col_cos, col_sin, row_cos, row_sin, twist_cos, twist_sin = tables
    outer_real = jnp.einsum("pk,bkj->bpj", row_cos, held_real, precision=highest) - jnp.einsum(
        "pk,bkj->bpj", row_sin, held_imag, precision=highest
    )
    outer_imag = jnp.einsum("pk,bkj->bpj", row_cos, held_imag, precision=highest) + jnp.einsum(
        "pk,bkj->bpj", row_sin, held_real, precision=highest
    )
    back_real = outer_real * twist_cos - outer_imag * twist_sin
    back_imag = outer_real * twist_sin + outer_imag * twist_cos
    series = jnp.einsum("qk,bpk->bqp", col_cos, back_real, precision=highest) - jnp.einsum(
        "qk,bpk->bqp", col_sin, back_imag, precision=highest
    )
    return (series / length).reshape(held_real.shape[0], length)


def wiener(amplitude, noise_power):
    dish_local = amplitude.shape[0]
    owned_modes = amplitude.shape[1]
    length = amplitude.shape[2]
    columns = length // 128
    col_cos, col_sin = dft_table(columns)
    row_cos, row_sin = dft_table(128)
    twist_cos, twist_sin = twist_table(128, columns)
    tables = (col_cos, col_sin, row_cos, row_sin, twist_cos, twist_sin)
    spec_real, spec_imag = forward(amplitude.reshape(dish_local * owned_modes, length), tables)
    squared = spec_real * spec_real + spec_imag * spec_imag
    power_here = jnp.sum(squared.reshape(dish_local, owned_modes, 128, columns), axis=0)
    power_total = taken_together(power_here.astype(jnp.bfloat16), "dish").astype(jnp.float32)
    power = power_total / float(dish_local * lax.axis_size("dish") * length)
    gain = power / (power + noise_power.reshape(owned_modes, 128, columns))
    gain_rows = gain[None].reshape(dish_local * owned_modes, 128, columns)
    signal = inverse(spec_real * gain_rows, spec_imag * gain_rows, tables, length)
    return signal.reshape(dish_local, owned_modes, length)


def body(sky_data, eigenmodes, noise_power):
    channels = sky_data.shape[1]
    position = lax.axis_index(BLK)
    local_modes = lax.dynamic_slice_in_dim(eigenmodes, position * channels, channels, 0)
    picked = local_modes
    summed = sum_by_axis(
        jnp.einsum("cm,dct->mdt", picked, sky_data, precision=highest),
        (("blk_0", "blk_1"), "blk_2"),
        0,
    )
    owned_amplitude = jnp.transpose(summed, (1, 0, 2))
    signal = wiener(owned_amplitude, noise_power)
    picked = local_modes
    fitted = jnp.einsum(
        "cm,dmt->dct", picked, lax.all_gather(signal, BLK, axis=1, tiled=True), precision=highest
    )
    cleaned = (sky_data - fitted).astype(jnp.bfloat16)
    return (cleaned, signal)


def solution(mesh):
    finer = Mesh(
        mesh.devices.reshape(mesh.shape["dish"], 2, 8, 2), ("dish", "blk_0", "blk_1", "blk_2")
    )
    return jax.shard_map(
        body,
        mesh=finer,
        in_specs=(P("dish", BLK, None), P(), P(BLK, None)),
        out_specs=(P("dish", BLK, None), P("dish", BLK, None)),
        check_vma=False,
    )
```

profile of v0, /device:TPU:1, one launch (start us, length us, event | category | flops | bytes accessed | tf_op | source)
XLA Modules:
  0.0 277.2 jit_solution(2609861436061905775)
XLA Ops:
  7.2 1.0 copy-done
  8.3 10.1 %convolution_bitcast_fusion.1 = f32[2,16,2,1,32768]{4,1,2,3,0:T(8,128)S(1)} fusion(f32[1,64,32768]{2,1,0:T(8,128)} %param.3, f32[16,2,2,64]{3,2,1,0:T(2,128)S(1)} %bitcast.85), kind=kOutput, calls=%fused_computation.1 | convolution fusion | flops 1610612736 | bytes 16793600 | tf_op jit(solution)/shard_map/cm,dct->mdt/dot_general | solution.py:115
  18.4 13.3 %all_to_all.15 = f32[2,16,2,1,32768]{4,1,2,3,0:T(8,128)S(1)} all-to-all(f32[2,16,2,1,32768]{4,1,2,3,0:T(8,128)S(1)} %convolution_bitcast_fusion.1), channel_id=1, replica_groups=mesh['dish'=8,'blk_0'=2,'blk_1'=8,'blk_2'=2] {'blk_2'}, dimensions={0} | all-to-all | bytes 16777216 | tf_op jit(solution)/shard_map/all_to_all | solution.py:28
  31.7 0.7 bitcast_reduce_fusion
  32.5 5.2 %copy.49 = f32[16,2,1,32768]{3,1,2,0:T(2,128)} copy(f32[16,2,1,32768]{3,0,1,2:T(8,128)S(1)} %bitcast.82) | data formatting | bytes 8388608 | tf_op jit(solution)/shard_map/reduce_sum | solution.py:29
  37.7 7.6 %all-to-all-start.1 = ((f32[16,2,1,32768]{3,1,2,0:T(2,128)}), f32[16,2,1,32768]{3,1,2,0:T(2,128)}, u32[]{:S(2)}, u32[]{:S(2)}) async-start(f32[16,2,1,32768]{3,1,2,0:T(2,128)} %copy.49), calls=%async_computation.1 | async-start | bytes 8388608 | tf_op jit(solution)/shard_map/all_to_all | solution.py:36
  45.8 94.2 %all-to-all-done.1 = f32[16,2,1,32768]{3,1,2,0:T(2,128)} async-done(((f32[16,2,1,32768]{3,1,2,0:T(2,128)}), f32[16,2,1,32768]{3,1,2,0:T(2,128)}, u32[]{:S(2)}, u32[]{:S(2)}) %all-to-all-start.1) | async-done | bytes 4194336 | tf_op jit(solution)/shard_map/all_to_all | solution.py:36
  140.0 3.6 %reduce_sum.35 = f32[2,32768]{1,0:T(2,128)S(1)} reduce(f32[16,2,1,32768]{3,1,2,0:T(2,128)} %all-to-all-done.1, f32[]{:T(128)} %constant.66.clone.1), dimensions={0,2}, to_apply=%region_1.0 | reduce | flops 983040 | bytes 4456452 | tf_op jit(solution)/shard_map/reduce_sum | solution.py:37
  143.6 1.5 convolution_negate_fusion
  145.1 1.5 fusion.15
  146.6 0.8 fusion.66
  147.3 0.8 fusion.64
  148.1 0.8 fusion.10
  148.9 0.8 add_convert_fusion
  149.8 1.1 broadcast_in_dim.2
  150.9 6.3 %all-to-all-start.2 = ((bf16[8,2,128,256]{3,2,1,0:T(8,128)(2,1)}), bf16[8,2,128,256]{3,2,1,0:T(8,128)(2,1)S(1)}, u32[]{:S(2)}, u32[]{:S(2)}) async-start(bf16[8,2,128,256]{3,2,1,0:T(8,128)(2,1)} %broadcast_in_dim.2), calls=%async_computation.2 | async-start | bytes 2097152 | tf_op jit(solution)/shard_map/all_to_all | solution.py:14
  157.6 14.9 %all-to-all-done.2 = bf16[8,2,128,256]{3,2,1,0:T(8,128)(2,1)S(1)} async-done(((bf16[8,2,128,256]{3,2,1,0:T(8,128)(2,1)}), bf16[8,2,128,256]{3,2,1,0:T(8,128)(2,1)S(1)}, u32[]{:S(2)}, u32[]{:S(2)}) %all-to-all-start.2) | async-done | bytes 1048608 | tf_op jit(solution)/shard_map/all_to_all | solution.py:14
  174.2 0.7 fusion.8
  175.5 1.4 fusion.19
  176.9 1.4 fusion.6
  178.2 0.8 copy.63
  179.1 1.8 reshape_reshape.4
  180.9 70.9 %all-gather.2.cloned.1.call-done = f32[1,64,32768]{2,0,1:T(1,128)} async-done(((f32[1,2,32768]{2,0,1:T(1,128)}), f32[1,64,32768]{2,0,1:T(1,128)}) %all-gather.2.cloned.1.call-update) | async-done | bytes 8388624 | tf_op jit(solution)/shard_map/all_gather | solution.py:123
  251.9 18.5 %fusion.1 = bf16[1,64,32768]{2,1,0:T(8,128)(2,1)} fusion(f32[1,64,32768]{2,1,0:T(8,128)} %param.3, f32[64,64]{0,1:T(8,128)S(1)} %constant_dynamic-slice_fusion, f32[1,64,32768]{2,0,1:T(1,128)} %all-gather.2.cloned.1.call-done), kind=kOutput, calls=%fused_computation.3 | convolution fusion | flops 1614807040 | bytes 20987904 | tf_op jit(solution)/shard_map/cm,dmt->dct/dot_general | solution.py:122
  (16 shorter events, 3.4 us)
Async XLA Ops:
  7.2 1.0 copy-start
  37.7 102.3 %all-to-all-start.1 = ((f32[16,2,1,32768]{3,1,2,0:T(2,128)}), f32[16,2,1,32768]{3,1,2,0:T(2,128)}, u32[]{:S(2)}, u32[]{:S(2)}) async-start(f32[16,2,1,32768]{3,1,2,0:T(2,128)} %copy.49), calls=%async_computation.1 | async-start | bytes 8388608 | tf_op jit(solution)/shard_map/all_to_all | solution.py:36
  45.3 112.2 %copy-start.1 = (f32[2,32768]{1,0:T(2,128)S(1)}, f32[2,32768]{1,0:T(2,128)}, u32[]{:S(2)}) copy-start(f32[2,32768]{1,0:T(2,128)} %param.5) | copy-start | bytes 786436
  150.9 21.7 %all-to-all-start.2 = ((bf16[8,2,128,256]{3,2,1,0:T(8,128)(2,1)}), bf16[8,2,128,256]{3,2,1,0:T(8,128)(2,1)S(1)}, u32[]{:S(2)}, u32[]{:S(2)}) async-start(bf16[8,2,128,256]{3,2,1,0:T(8,128)(2,1)} %broadcast_in_dim.2), calls=%async_computation.2 | async-start | bytes 2097152 | tf_op jit(solution)/shard_map/all_to_all | solution.py:14
  157.2 94.7 %all-gather.2.cloned.1.call-start = ((), (), s32[]{:S(2)}) async-start(), calls=%async_computation.3 | async-start | bytes 8650752 | tf_op jit(solution)/shard_map/all_gather | solution.py:123
Sparse Core Ops, SparseCore 0:
  179.2 72.5 all-gather.1
where the time goes:
time: 278 us; the launch traced here: 277 us
  waiting for transfers between devices  180 us (65%)
  matrix products  40 us (14%)
  starting transfers between devices  14.2 us (5%)
  between operations  14.2 us (5%)
  blocking collectives  13.3 us (5%)
  local copies, waits for them, and re-layouts  10.5 us (4%)
  other arithmetic  5.01 us (2%)
    all_to_all x1, waiting for transfers between devices, sum_by_axis(): lax.all_to_all(nearer, far, split_axis=0, concat_axis=0, tiled=True)  94.2 us
    all_gather x1, waiting for transfers between devices, body(): lax.all_gather(signal, BLK, axis=1, tiled=True)  70.9 us
    dot_general x1, matrix products, body(): jnp.einsum('cm,dmt->dct', picked, lax.all_gather(signal, BLK, axis=1, til...  18.5 us
    all_to_all x1, waiting for transfers between devices, sent_to_all(): return lax.all_to_all(copies, axis, split_axis=0, concat_axis=0, tiled=True)  14.9 us
    all_to_all x1, blocking collectives, sent_and_summed(): parts = lax.all_to_all(in_blocks(value, dim, size), axis, 0, 0, tiled=True)  13.3 us
    dot_general x1, matrix products, body(): jnp.einsum('cm,dct->mdt', picked, sky_data, precision=highest)  10.1 us
    all_to_all x1, starting transfers between devices, sum_by_axis(): lax.all_to_all(nearer, far, split_axis=0, concat_axis=0, tiled=True)  7.58 us
    all_to_all x1, starting transfers between devices, sent_to_all(): return lax.all_to_all(copies, axis, split_axis=0, concat_axis=0, tiled=True)  6.33 us
  transfers between devices with their start and end apart: 3, of which 3 were waited for; matrix products, arithmetic and copies ran while one was open for 1% of the time, Pallas kernels for 0%

commit v1 on v0

--- a/solution.py
+++ b/solution.py
@@ -7,6 +7,13 @@
 
 BLK = ("blk_0", "blk_1", "blk_2")
 highest = lax.Precision.HIGHEST
+
+
+def swapped_in(block, axis, dim):
+    size = lax.axis_size(axis)
+    blocks = jnp.stack([block for _ in range(size)])
+    blocks = lax.all_to_all(blocks, axis, split_axis=0, concat_axis=0)
+    return jnp.concatenate(blocks, axis=dim)
 
 
 def sent_to_all(value, axis):
@@ -119,9 +126,7 @@
     owned_amplitude = jnp.transpose(summed, (1, 0, 2))
     signal = wiener(owned_amplitude, noise_power)
     picked = local_modes
-    fitted = jnp.einsum(
-        "cm,dmt->dct", picked, lax.all_gather(signal, BLK, axis=1, tiled=True), precision=highest
-    )
+    fitted = jnp.einsum("cm,dmt->dct", picked, swapped_in(signal, BLK, 1), precision=highest)
     cleaned = (sky_data - fitted).astype(jnp.bfloat16)
     return (cleaned, signal)
 

time: 278 us -> 400 us (1.44)
  waiting for transfers between devices: 180 us -> 293 us
  local copies, waits for them, and re-layouts: 10.5 us -> 26.9 us
  between operations: 14.2 us -> 0.85 us
  starting transfers between devices: 14.2 us -> 25.1 us
  matrix products: 40 us -> 34.3 us
    all_to_all x0 -> x1, waiting for transfers between devices: none -> 183 us  [swapped_in(): blocks = lax.all_to_all(blocks, axis, split_axis=0, concat_axis=0)]
    all_gather x1 -> x0, waiting for transfers between devices: 70.9 us -> none  [body(): lax.all_gather(signal, BLK, axis=1, tiled=True)]
    another operation x0 -> x2, local copies, waits for them, and re-layouts: none -> 17.9 us
    all_to_all x0 -> x1, starting transfers between devices: none -> 11.1 us  [swapped_in(): blocks = lax.all_to_all(blocks, axis, split_axis=0, concat_axis=0)]
    dot_general x1, matrix products: 18.5 us -> 12.8 us  [body(): jnp.einsum('cm,dmt->dct', picked, swapped_in(signal, BLK, 1), precision=h...]
  transfers between devices with their start and end apart: 3 -> 3, of which waited for: 3 -> 3; matrix products, arithmetic and copies ran while one was open for 1% -> 0% of each run, Pallas kernels for 0% -> 0%
where the time goes in v1:
time: 400 us; the launch traced here: 398 us
  waiting for transfers between devices  293 us (73%)
  matrix products  34.3 us (9%)
  local copies, waits for them, and re-layouts  26.9 us (7%)
  starting transfers between devices  25.1 us (6%)
  blocking collectives  13.3 us (3%)
  other arithmetic  5.01 us (1%)
    all_to_all x1, waiting for transfers between devices, swapped_in(): blocks = lax.all_to_all(blocks, axis, split_axis=0, concat_axis=0)  183 us
    all_to_all x1, waiting for transfers between devices, sum_by_axis(): lax.all_to_all(nearer, far, split_axis=0, concat_axis=0, tiled=True)  94.2 us
    all_to_all x1, waiting for transfers between devices, sent_to_all(): return lax.all_to_all(copies, axis, split_axis=0, concat_axis=0, tiled=True)  15.2 us
    all_to_all x1, blocking collectives, sent_and_summed(): parts = lax.all_to_all(in_blocks(value, dim, size), axis, 0, 0, tiled=True)  13.3 us
    dot_general x1, matrix products, body(): jnp.einsum('cm,dmt->dct', picked, swapped_in(signal, BLK, 1), precision=h...  12.8 us
    all_to_all x1, starting transfers between devices, swapped_in(): blocks = lax.all_to_all(blocks, axis, split_axis=0, concat_axis=0)  11.1 us
    another operation x1, local copies, waits for them, and re-layouts  10.9 us
    dot_general x1, matrix products, body(): jnp.einsum('cm,dct->mdt', picked, sky_data, precision=highest)  10.1 us
  transfers between devices with their start and end apart: 3, of which 3 were waited for; matrix products, arithmetic and copies ran while one was open for 0% of the time, Pallas kernels for 0%

profile of v1, /device:TPU:1, one launch (start us, length us, event | category | flops | bytes accessed | tf_op | source)
XLA Modules:
  0.0 397.9 jit_solution(13100780893684145278)
XLA Ops:
  0.7 1.0 copy-done
  1.8 10.1 %convolution_bitcast_fusion.1 = f32[2,16,2,1,32768]{4,1,2,3,0:T(8,128)S(1)} fusion(f32[1,64,32768]{2,1,0:T(8,128)} %param.3, f32[16,2,2,64]{3,2,1,0:T(2,128)S(1)} %bitcast.87), kind=kOutput, calls=%fused_computation.1 | convolution fusion | flops 1610612736 | bytes 16793600 | tf_op jit(solution)/shard_map/cm,dct->mdt/dot_general | solution.py:122
  11.9 13.3 %all_to_all.20 = f32[2,16,2,1,32768]{4,1,2,3,0:T(8,128)S(1)} all-to-all(f32[2,16,2,1,32768]{4,1,2,3,0:T(8,128)S(1)} %convolution_bitcast_fusion.1), channel_id=1, replica_groups=mesh['dish'=8,'blk_0'=2,'blk_1'=8,'blk_2'=2] {'blk_2'}, dimensions={0} | all-to-all | bytes 16777216 | tf_op jit(solution)/shard_map/all_to_all | solution.py:35
  25.9 5.2 %copy.50 = f32[16,2,1,32768]{3,1,2,0:T(2,128)} copy(f32[16,2,1,32768]{3,0,1,2:T(8,128)S(1)} %bitcast.83) | data formatting | bytes 8388608 | tf_op jit(solution)/shard_map/reduce_sum | solution.py:36
  31.2 7.6 %all-to-all-start.1 = ((f32[16,2,1,32768]{3,1,2,0:T(2,128)}), f32[16,2,1,32768]{3,1,2,0:T(2,128)}, u32[]{:S(2)}, u32[]{:S(2)}) async-start(f32[16,2,1,32768]{3,1,2,0:T(2,128)} %copy.50), calls=%async_computation.1 | async-start | bytes 8388608 | tf_op jit(solution)/shard_map/all_to_all | solution.py:43
  39.3 94.2 %all-to-all-done.1 = f32[16,2,1,32768]{3,1,2,0:T(2,128)} async-done(((f32[16,2,1,32768]{3,1,2,0:T(2,128)}), f32[16,2,1,32768]{3,1,2,0:T(2,128)}, u32[]{:S(2)}, u32[]{:S(2)}) %all-to-all-start.1) | async-done | bytes 4194336 | tf_op jit(solution)/shard_map/all_to_all | solution.py:43
  133.5 3.6 reduce_sum.35
  137.1 1.5 convolution_negate_fusion
  138.5 1.5 fusion.13
  140.0 0.8 fusion.64
  140.8 0.8 fusion.62
  141.6 0.8 fusion.8
  142.3 0.8 add_convert_fusion
  143.2 1.1 broadcast_in_dim.2
  144.3 6.4 %all-to-all-start.2 = ((bf16[8,2,128,256]{3,2,1,0:T(8,128)(2,1)}), bf16[8,2,128,256]{3,2,1,0:T(8,128)(2,1)S(1)}, u32[]{:S(2)}, u32[]{:S(2)}) async-start(bf16[8,2,128,256]{3,2,1,0:T(8,128)(2,1)} %broadcast_in_dim.2), calls=%async_computation.2 | async-start | bytes 2097152 | tf_op jit(solution)/shard_map/all_to_all | solution.py:21
  150.8 15.2 %all-to-all-done.2 = bf16[8,2,128,256]{3,2,1,0:T(8,128)(2,1)S(1)} async-done(((bf16[8,2,128,256]{3,2,1,0:T(8,128)(2,1)}), bf16[8,2,128,256]{3,2,1,0:T(8,128)(2,1)S(1)}, u32[]{:S(2)}, u32[]{:S(2)}) %all-to-all-start.2) | async-done | bytes 1048608 | tf_op jit(solution)/shard_map/all_to_all | solution.py:21
  168.9 1.4 fusion.17
  170.3 1.4 fusion.4
  172.0 7.0 %stack.3 = f32[32,1,2,32768]{3,2,1,0:T(2,128)} broadcast(f32[2,32768]{1,0:T(2,128)S(1)} %bitcast.85), dimensions={2,3} | broadcast | bytes 8650752 | tf_op jit(solution)/shard_map/stack | solution.py:14
  179.0 11.1 %all-to-all-start.3 = ((f32[32,1,2,32768]{3,2,1,0:T(2,128)}), f32[32,1,2,32768]{3,2,1,0:T(2,128)}, u32[]{:S(2)}, u32[]{:S(2)}) async-start(f32[32,1,2,32768]{3,2,1,0:T(2,128)} %stack.3), calls=%async_computation.3 | async-start | bytes 16777216 | tf_op jit(solution)/shard_map/all_to_all | solution.py:15
  190.2 0.9 reshape_reshape.4
  191.0 183.2 %all-to-all-done.3 = f32[32,1,2,32768]{3,2,1,0:T(2,128)} async-done(((f32[32,1,2,32768]{3,2,1,0:T(2,128)}), f32[32,1,2,32768]{3,2,1,0:T(2,128)}, u32[]{:S(2)}, u32[]{:S(2)}) %all-to-all-start.3) | async-done | bytes 8388640 | tf_op jit(solution)/shard_map/all_to_all | solution.py:15
  374.2 10.9 %reshape.71 = f32[64,32768]{1,0:T(8,128)} reshape(f32[32,1,2,32768]{3,2,1,0:T(2,128)} %all-to-all-done.3) | data formatting | bytes 16777216 | tf_op jit(solution)/shard_map/reshape.10
  385.1 12.8 %fusion.1 = bf16[1,64,32768]{2,1,0:T(8,128)(2,1)} fusion(f32[1,64,32768]{2,1,0:T(8,128)} %param.3, f32[64,32768]{1,0:T(8,128)} %reshape.71, f32[64,64]{0,1:T(8,128)S(1)} %constant_dynamic-slice_fusion), kind=kOutput, calls=%fused_computation.3 | convolution fusion | flops 1614807040 | bytes 20987904 | tf_op jit(solution)/shard_map/cm,dmt->dct/dot_general | solution.py:129
  (20 shorter events, 4.8 us)
Async XLA Ops:
  0.6 1.1 copy-start
  31.2 102.3 %all-to-all-start.1 = ((f32[16,2,1,32768]{3,1,2,0:T(2,128)}), f32[16,2,1,32768]{3,1,2,0:T(2,128)}, u32[]{:S(2)}, u32[]{:S(2)}) async-start(f32[16,2,1,32768]{3,1,2,0:T(2,128)} %copy.50), calls=%async_computation.1 | async-start | bytes 8388608 | tf_op jit(solution)/shard_map/all_to_all | solution.py:43
  38.8 111.9 %copy-start.2 = (f32[2,32768]{1,0:T(2,128)S(1)}, f32[2,32768]{1,0:T(2,128)}, u32[]{:S(2)}) copy-start(f32[2,32768]{1,0:T(2,128)} %param.5) | copy-start | bytes 786436
  144.3 21.7 %all-to-all-start.2 = ((bf16[8,2,128,256]{3,2,1,0:T(8,128)(2,1)}), bf16[8,2,128,256]{3,2,1,0:T(8,128)(2,1)S(1)}, u32[]{:S(2)}, u32[]{:S(2)}) async-start(bf16[8,2,128,256]{3,2,1,0:T(8,128)(2,1)} %broadcast_in_dim.2), calls=%async_computation.2 | async-start | bytes 2097152 | tf_op jit(solution)/shard_map/all_to_all | solution.py:21
  179.0 195.2 %all-to-all-start.3 = ((f32[32,1,2,32768]{3,2,1,0:T(2,128)}), f32[32,1,2,32768]{3,2,1,0:T(2,128)}, u32[]{:S(2)}, u32[]{:S(2)}) async-start(f32[32,1,2,32768]{3,2,1,0:T(2,128)} %stack.3), calls=%async_computation.3 | async-start | bytes 16777216 | tf_op jit(solution)/shard_map/all_to_all | solution.py:15
  385.1 12.8 %copy-start.1 = (f32[2048,64]{0,1:T(8,128)S(1)}, f32[2048,64]{0,1:T(8,128)}, u32[]{:S(2)}) copy-start(f32[2048,64]{0,1:T(8,128)} %param.4) | copy-start | bytes 1572868
